TPU v7x, 32 devices: a whole 2x2x4 slice. The times are simulated.
32 devices in a mesh: groups: 2 (over y), seq: 8 (over z, x), section: 2 (over core).
Axes of the slice: x: 2, y: 2, z: 4, core: 2. Of those that a mesh axis runs over, the one named last changes fastest.
Arguments:
- skip_in: bfloat16 [2, 1024, 1536], P('groups', 'seq'), parts along dimension 0, may hold values from -6 to 6
- attn_gain: float32 [1536], replicated, may hold values from 0.25 to 1.75
- query_weight: bfloat16 [1536, 1024], P(None, 'section'), may hold values from -0.625 to 0.625
- kv_weight: bfloat16 [1536, 256], replicated, may hold values from -0.15625 to 0.15625
- pair_bias: float32 [2, 8, 32, 32], P('groups', 'section', 'seq'), parts along dimension 0, may hold values from -12 to 400
- out_weight: bfloat16 [1024, 1536], P('section'), may hold values from -0.1875 to 0.1875
- dec_gain: float32 [1536], replicated, may hold values from 0.25 to 1.75
- dec_weight: bfloat16 [5, 1536, 768], P(None, 'seq', 'section'), may hold values from -0.0625 to 0.0625
- dec_bias: float32 [768], P('section'), may hold values from -3 to 3
Outputs:
- decoded: bfloat16 [2, 1024, 768], P('groups', 'seq', 'section'), parts along dimension 0
There are 2 independent parts, one for each index of `groups`. A program takes and returns all parts, laid end to end along the dimension named above; an argument that names none is the same for every part. Nothing has to cross between parts.
All inputs are finite; a program needn't handle non-finite values.
Results may differ from a plain program's by a relative error of at most 0.0095.
Values may be sent and summed in bfloat16 or wider, within the bound.
No kernel may reach another device: no remote copies, remote signals or barrier semaphores. Data moves between devices by JAX's collectives and lax.ppermute only.
A program may use at most 64 MiB of HBM per device.

v0:
```python
import math
import jax
import jax.numpy as jnp
from jax import lax
from jax.sharding import PartitionSpec as P

HEAD = 128
KW = 5
PAIR = 16


def extended(block, sides, width):
    for axis, dim in sides:
        count = lax.axis_size(axis)
        forward = [(i, i + 1) for i in range(count - 1)]
        backward = [(target, source) for source, target in forward]
        low = lax.ppermute(
            lax.slice_in_dim(block, block.shape[dim] - width, None, axis=dim), axis, forward
        )
        high = lax.ppermute(lax.slice_in_dim(block, 0, width, axis=dim), axis, backward)
        block = jnp.concatenate([low, block, high], axis=dim)
    return block


def norm_scale(values_in, gain):
    wide = values_in.astype(jnp.float32)
    return wide * lax.rsqrt(jnp.mean(wide * wide, axis=-1, keepdims=True) + 1e-06) * gain


def body(
    skip_in,
    attn_gain,
    query_weight,
    kv_weight,
    pair_bias,
    out_weight,
    dec_gain,
    dec_weight,
    dec_bias,
):
    seq_count, local_rows, channels = skip_in.shape
    half_rows = local_rows // 2
    local_heads = query_weight.shape[1] // HEAD
    logit_scale = 1.0 / math.sqrt(HEAD)
    pooled = jnp.max(skip_in.reshape(seq_count, half_rows, 2, channels), axis=2)
    normed = norm_scale(pooled, attn_gain).astype(jnp.bfloat16)
    flattened = normed.reshape(seq_count * half_rows, channels)
    query_rows = jnp.dot(flattened, query_weight, preferred_element_type=jnp.float32).astype(
        jnp.bfloat16
    )
    query_rows = query_rows.reshape(seq_count, half_rows, local_heads, HEAD)
    row_bias = jnp.repeat(pair_bias, PAIR, axis=2)
    row_bias = jnp.pad(row_bias, ((0, 0), (0, 0), (0, 0), (0, 2)))
    quarter = half_rows // 2
    own_rows = lax.dynamic_slice_in_dim(normed, lax.axis_index("section") * quarter, quarter, 1)
    key_values = jnp.dot(
        own_rows.reshape(seq_count * quarter, channels),
        kv_weight,
        preferred_element_type=jnp.float32,
    )
    key_values = key_values.astype(jnp.bfloat16).reshape(seq_count, quarter, 2 * HEAD)
    piece = lax.all_gather(key_values, ("seq", "section"), axis=1, tiled=True)
    start = jnp.int32(0)
    running_max = jnp.full((seq_count, local_heads, half_rows), -1e30, jnp.float32)
    running_sum = jnp.zeros((seq_count, local_heads, half_rows), jnp.float32)
    weighted = jnp.zeros((seq_count, local_heads, half_rows, HEAD), jnp.float32)
    piece_rows = piece.shape[1]
    block_size = min(piece_rows, 2048)
    for offset in range(0, piece_rows, block_size):
        piece_len = min(block_size, piece_rows - offset)
        sub_piece = piece[:, offset : offset + piece_len]
        key_portion = sub_piece[:, :, :HEAD]
        value_part = sub_piece[:, :, HEAD:]
        first_row = start + offset
        blocks = lax.dynamic_slice_in_dim(row_bias, first_row // PAIR, piece_len // PAIR + 2, 3)
        spread = jnp.repeat(blocks, PAIR, axis=3)
        key_bias = lax.dynamic_slice_in_dim(spread, first_row % PAIR, piece_len, 3)
        scores = (
            jnp.einsum(
                "wtzj,wgj->wztg", query_rows, key_portion, preferred_element_type=jnp.float32
            )
            * logit_scale
            + key_bias
        )
        new_max = jnp.maximum(running_max, jnp.max(scores, axis=-1))
        rescale = jnp.exp(running_max - new_max)
        exponent_scores = jnp.exp(scores - new_max[..., None])
        running_sum = running_sum * rescale + jnp.sum(exponent_scores, axis=-1)
        weighted = weighted * rescale[..., None] + jnp.einsum(
            "umrl,ult->umrt",
            exponent_scores.astype(jnp.bfloat16),
            value_part,
            preferred_element_type=jnp.float32,
        )
        running_max = new_max
    folded = (running_max, running_sum, weighted)
    running_max, running_sum, weighted = folded
    context = (weighted / running_sum[..., None]).astype(jnp.bfloat16)
    context = jnp.transpose(context, (0, 2, 1, 3)).reshape(
        seq_count * half_rows, local_heads * HEAD
    )
    partial_value = jnp.dot(context, out_weight, preferred_element_type=jnp.float32).reshape(
        seq_count, half_rows, channels
    )
    summed = lax.psum(partial_value.astype(jnp.bfloat16), "section").astype(jnp.float32)
    attended = (pooled.astype(jnp.float32) + summed).astype(jnp.bfloat16)
    joined = (
        jnp.repeat(attended, 2, axis=1).astype(jnp.float32) + skip_in.astype(jnp.float32)
    ).astype(jnp.bfloat16)
    activated = jax.nn.gelu(norm_scale(joined, dec_gain)).astype(jnp.bfloat16)
    padded = extended(activated, (("seq", 1),), KW // 2)
    out_half = dec_weight.shape[2]
    piece = lax.all_gather(dec_weight, "seq", axis=1, tiled=True)
    piece_rows = piece.shape[1]
    stacked = jnp.concatenate(
        [padded[:, tap_index : tap_index + local_rows] for tap_index in range(KW)], axis=2
    )
    stacked = stacked.reshape(seq_count * local_rows, KW * piece_rows)
    convolved = jnp.dot(
        stacked, piece.reshape(KW * piece_rows, out_half), preferred_element_type=jnp.float32
    )
    residual = lax.dynamic_slice_in_dim(joined, lax.axis_index("section") * out_half, out_half, 2)
    decoded = (
        convolved.reshape(seq_count, local_rows, out_half) + dec_bias + residual.astype(jnp.float32)
    )
    return decoded.astype(jnp.bfloat16)


def solution(mesh):
    return jax.shard_map(
        body,
        mesh=mesh,
        in_specs=(
            P("groups", "seq", None),
            P(),
            P(None, "section"),
            P(),
            P("groups", "section", "seq", None),
            P("section", None),
            P(),
            P(None, "seq", "section"),
            P("section"),
        ),
        out_specs=P("groups", "seq", "section"),
        check_vma=False,
    )
```

profile of v0, /device:TPU:0, one launch (start us, length us, event | category | flops | bytes accessed | tf_op | source)
XLA Modules:
  0.0 150.7 jit_solution(8483585687084230014)
XLA Ops:
  7.4 2.0 %reshape.220 = bf16[64,2,1536]{2,1,0:T(2,128)(2,1)} reshape(bf16[1,128,1536]{2,1,0:T(8,128)(2,1)} %param.9) | data formatting | bytes 786432 | tf_op jit(solution)/shard_map/reshape | solution.py:45
  9.4 2.0 %reduce_max.18 = bf16[64,1536]{1,0:T(8,128)(2,1)S(1)} reduce(bf16[64,2,1536]{2,1,0:T(2,128)(2,1)} %reshape.220, bf16[]{:T(256)} %constant.24.clone.1), dimensions={1}, to_apply=%region_0.0 | reduce | flops 98304 | bytes 589826 | tf_op jit(solution)/shard_map/reduce_max | solution.py:45
  11.5 0.8 convert_bitcast_fusion
  12.4 1.5 %convolution_convert_fusion.2 = bf16[32,256]{1,0:T(8,128)(2,1)S(1)} fusion(bf16[1536,256]{1,0:T(8,128)(2,1)} %param.12, f32[1,64,1536]{2,1,0:T(8,128)} %convert_bitcast_fusion, s32[]{:T(128)S(6)} %select_n.15, f32[1536]{0:T(1024)S(1)} %copy-done.2, f32[32]{0:T(128)S(1)} %dynamic-slice.1), kind=kOutput, calls=%fused_computation.18 | convolution fusion | flops 25321472 | bytes 1005700 | tf_op jit(solution)/shard_map/dot_general | solution.py:56
  13.9 25.2 %all-gather = bf16[512,256]{1,0:T(8,128)(2,1)} all-gather(bf16[32,256]{1,0:T(8,128)(2,1)S(1)} %convolution_convert_fusion.2), channel_id=2, replica_groups=mesh['groups'=2,'seq'=8,'section'=2] {'seq','section'}, dimensions={0}, use_global_device_ids=true | all-gather | bytes 278528 | tf_op jit(solution)/shard_map/all_gather | solution.py:62
  39.1 0.4 fusion.19
  40.2 1.2 fusion.63
  41.7 1.2 fusion.20
  42.9 1.1 fusion
  44.1 0.5 all-gather.3.cloned.1.call-update
  44.6 15.0 %all-reduce.3.cloned.1.call-done = bf16[1,64,1536]{2,1,0:T(8,128)(2,1)} async-done(((bf16[1,64,1536]{2,1,0:T(8,128)(2,1)}), bf16[1,64,1536]{2,1,0:T(8,128)(2,1)}) %all-reduce.3.cloned.1.call-update) | async-done | bytes 196624 | tf_op jit(solution)/shard_map/psum | solution.py:105
  59.6 1.0 fusion.46
  60.9 0.5 convert_element_type.120
  61.4 1.2 fusion.21
  63.0 3.6 %collective-permute-start = (bf16[1,2,1536]{2,1,0:T(2,128)(2,1)S(1)}, bf16[1,2,1536]{2,1,0:T(2,128)(2,1)S(1)}, u32[]{:S(2)}, u32[]{:S(2)}) collective-permute-start(bf16[1,2,1536]{2,1,0:T(2,128)(2,1)S(1)} %get-tuple-element.8), channel_id=1, source_target_pairs={{0,2},{2,4},{4,6},{6,8},{8,10},{10,12},{12,14},{1,3},{3,5},{5,7},{... | collective-permute-start | bytes 18440 | tf_op jit(solution)/shard_map/ppermute | solution.py:17
  66.7 1.3 collective-permute-start.1
  68.0 0.8 fusion.36
  68.8 0.9 fusion.41
  69.7 1.2 constant_dynamic-update-slice_fusion
  70.9 1.3 collective-permute-done.1
  72.2 0.9 fusion.34
  73.1 0.9 fusion.40
  74.0 64.1 %all-gather.3.cloned.1.call-done = bf16[5,1536,384]{2,1,0:T(8,128)(2,1)} async-done(((bf16[5,192,384]{2,1,0:T(8,128)(2,1)}), bf16[5,1536,384]{2,1,0:T(8,128)(2,1)}) %all-gather.3.cloned.1.call-update) | async-done | bytes 5898256 | tf_op jit(solution)/shard_map/all_gather | solution.py:113
  138.1 5.1 %fusion.14 = bf16[1,128,384]{2,1,0:T(8,128)(2,1)} fusion(bf16[7680,384]{1,0:T(8,128)(2,1)} %bitcast.79, bf16[1,128,7680]{2,1,0:T(8,128)(2,1)} %fusion.40, bf16[1,128,1536]{2,1,0:T(8,128)(2,1)S(1)} %get-tuple-element.6, s32[]{:T(128)S(6)} %select_n.16, f32[384]{0:T(512)S(1)} %copy-done.5), kind=kOutput, calls=%fused_computation.11 | convolution fusion | flops 755171328 | bytes 8062468 | tf_op jit(solution)/shard_map/dot_general | solution.py:119
  (33 shorter events, 1.9 us)
Async XLA Ops:
  7.4 35.6 %copy-start = (bf16[512,1536]{1,0:T(8,128)(2,1)S(1)}, bf16[512,1536]{1,0:T(8,128)(2,1)}, u32[]{:S(2)}) copy-start(bf16[512,1536]{1,0:T(8,128)(2,1)} %param.14) | copy-start | bytes 4718596
  7.4 5.0 %copy-start.2 = (f32[1536]{0:T(1024)S(1)}, f32[1536]{0:T(1024)}, u32[]{:S(2)}) copy-start(f32[1536]{0:T(1024)} %param.10) | copy-start | bytes 18436
  7.4 31.7 %copy-start.1 = (bf16[1536,512]{1,0:T(8,128)(2,1)S(1)}, bf16[1536,512]{1,0:T(8,128)(2,1)}, u32[]{:S(2)}) copy-start(bf16[1536,512]{1,0:T(8,128)(2,1)} %param.11) | copy-start | bytes 4718596
  7.4 52.2 %all-reduce.3.cloned.1.call-start = ((), (), s32[]{:S(2)}) async-start(), calls=%async_computation | async-start | bytes 393216 | tf_op jit(solution)/shard_map/psum | solution.py:105
  11.4 28.2 %copy-start.4 = (f32[1,4,4,32]{3,2,1,0:T(4,128)S(1)}, f32[1,4,4,32]{3,2,1,0:T(4,128)}, u32[]{:S(2)}) copy-start(f32[1,4,4,32]{3,2,1,0:T(4,128)} %param.13) | copy-start | bytes 6148
  44.0 94.0 %all-gather.3.cloned.1.call-start = ((), (), s32[]{:S(2)}) async-start(), calls=%async_computation.1 | async-start | bytes 6635520 | tf_op jit(solution)/shard_map/all_gather | solution.py:113
  60.6 2.1 %copy-start.3 = (f32[1536]{0:T(1024)S(1)}, f32[1536]{0:T(1024)}, u32[]{:S(2)}) copy-start(f32[1536]{0:T(1024)} %param.15) | copy-start | bytes 18436
  63.0 5.0 %collective-permute-start = (bf16[1,2,1536]{2,1,0:T(2,128)(2,1)S(1)}, bf16[1,2,1536]{2,1,0:T(2,128)(2,1)S(1)}, u32[]{:S(2)}, u32[]{:S(2)}) collective-permute-start(bf16[1,2,1536]{2,1,0:T(2,128)(2,1)S(1)} %get-tuple-element.8), channel_id=1, source_target_pairs={{0,2},{2,4},{4,6},{6,8},{8,10},{10,12},{12,14},{1,3},{3,5},{5,7},{... | collective-permute-start | bytes 18440 | tf_op jit(solution)/shard_map/ppermute | solution.py:17
  66.7 71.4 %copy-start.5 = (f32[384]{0:T(512)S(1)}, f32[384]{0:T(512)}, u32[]{:S(2)}) copy-start(f32[384]{0:T(512)} %param.17) | copy-start | bytes 4612
  66.7 5.5 %collective-permute-start.1 = (bf16[1,2,1536]{2,1,0:T(2,128)(2,1)S(1)}, bf16[1,2,1536]{2,1,0:T(2,128)(2,1)S(1)}, u32[]{:S(2)}, u32[]{:S(2)}) collective-permute-start(bf16[1,2,1536]{2,1,0:T(2,128)(2,1)S(1)} %get-tuple-element.7), channel_id=1, source_target_pairs={{2,0},{4,2},{6,4},{8,6},{10,8},{12,10},{14,12},{3,1},{5,3},{7,5},{... | collective-permute-start | bytes 18440 | tf_op jit(solution)/shard_map/ppermute | solution.py:20
Sparse Core Ops, SparseCore 0:
  44.2 15.3 all-reduce.2
Sparse Core Ops, SparseCore 1:
  46.7 91.3 all-gather.2
where the time goes:
time: 151 us
  waiting for transfers between devices  81 us (54%)
  blocking collectives  25.2 us (17%)
  between operations  15 us (10%)
  matrix products  10.6 us (7%)
  other arithmetic  10.3 us (7%)
  starting transfers between devices  4.96 us (3%)
  local copies, waits for them, and re-layouts  3.61 us (2%)
    all_gather x1, waiting for transfers between devices, body(): piece = lax.all_gather(dec_weight, 'seq', axis=1, tiled=True)  64.1 us
    all_gather x1, blocking collectives, body(): piece = lax.all_gather(key_values, ('seq', 'section'), axis=1, tiled=True)  25.2 us
    psum x1, waiting for transfers between devices, body(): lax.psum(partial_value.astype(jnp.bfloat16), 'section').astype(jnp.float32)  15 us
    dot_general x1, matrix products, body(): jnp.dot(stacked, piece.reshape(KW * piece_rows, out_half), preferred_elem...  5.14 us
    unnamed x4, other arithmetic  3.74 us
    ppermute x1, starting transfers between devices, extended(): lax.ppermute(lax.slice_in_dim(block, block.shape[dim] - width, None, axis...  3.62 us
  transfers between devices with their start and end apart: 4, of which 3 were waited for; matrix products, arithmetic and copies ran while one was open for 5% of the time, Pallas kernels for 0%

commit v1 on v0

--- a/solution.py
+++ b/solution.py
@@ -102,7 +102,9 @@
     partial_value = jnp.dot(context, out_weight, preferred_element_type=jnp.float32).reshape(
         seq_count, half_rows, channels
     )
-    summed = lax.psum(partial_value.astype(jnp.bfloat16), "section").astype(jnp.float32)
+    summed = jnp.sum(lax.all_gather(partial_value.astype(jnp.bfloat16), "section"), axis=0).astype(
+        jnp.float32
+    )
     attended = (pooled.astype(jnp.float32) + summed).astype(jnp.bfloat16)
     joined = (
         jnp.repeat(attended, 2, axis=1).astype(jnp.float32) + skip_in.astype(jnp.float32)

time: 151 us -> 120 us (0.79)
  waiting for transfers between devices: 81 us -> 58 us
  other arithmetic: 10.3 us -> 6.89 us
  matrix products: 10.6 us -> 8.13 us
  starting transfers between devices: 4.96 us -> 2.58 us
    psum x1 -> x0, waiting for transfers between devices: 15 us -> none  [body(): lax.psum(partial_value.astype(jnp.bfloat16), 'section').astype(jnp.float32)]
    all_gather x1, waiting for transfers between devices: 64.1 us -> 56 us  [body(): piece = lax.all_gather(dec_weight, 'seq', axis=1, tiled=True)]
    ppermute x1, starting transfers between devices: 3.62 us -> 1.29 us  [extended(): lax.ppermute(lax.slice_in_dim(block, block.shape[dim] - width, None, axis...]
    all_gather x0 -> x1, blocking collectives: none -> 2.09 us  [body(): lax.all_gather(partial_value.astype(jnp.bfloat16), 'section')]
  transfers between devices with their start and end apart: 4 -> 3, of which waited for: 3 -> 2; matrix products, arithmetic and copies ran while one was open for 5% -> 11% of each run, Pallas kernels for 0% -> 0%
where the time goes in v1:
time: 120 us; the launch traced here: 119 us
  waiting for transfers between devices  58 us (48%)
  blocking collectives  26.7 us (22%)
  between operations  13.6 us (11%)
  matrix products  8.13 us (7%)
  other arithmetic  6.89 us (6%)
  local copies, waits for them, and re-layouts  3.43 us (3%)
  starting transfers between devices  2.58 us (2%)
    all_gather x1, waiting for transfers between devices, body(): piece = lax.all_gather(dec_weight, 'seq', axis=1, tiled=True)  56 us
    all_gather x1, blocking collectives, body(): piece = lax.all_gather(key_values, ('seq', 'section'), axis=1, tiled=True)  24.6 us
    dot_general x1, matrix products, body(): jnp.dot(stacked, piece.reshape(KW * piece_rows, out_half), preferred_elem...  5.14 us
    unnamed x4, other arithmetic  3.83 us
  transfers between devices with their start and end apart: 3, of which 2 were waited for; matrix products, arithmetic and copies ran while one was open for 11% of the time, Pallas kernels for 0%

profile of v1, /device:TPU:0, one launch (start us, length us, event | category | flops | bytes accessed | tf_op | source)
XLA Modules:
  0.0 119.4 jit_solution(2956925508089055765)
XLA Ops:
  6.5 0.7 all-gather.4.cloned.1.call-update
  7.3 1.1 reshape.225
  8.4 0.7 broadcast_in_dim.29
  9.4 0.3 copy.19
  9.7 1.0 reduce_max.18
  11.1 1.6 %convolution_convert_fusion.2 = bf16[32,256]{1,0:T(8,128)(2,1)S(1)} fusion(bf16[1536,256]{1,0:T(8,128)(2,1)} %param.12, f32[1,64,1536]{2,1,0:T(8,128)S(1)} %convert_bitcast_fusion, s32[]{:T(128)S(6)} %select_n.15, f32[1536]{0:T(1024)S(1)} %copy-done.3, f32[32]{0:T(128)S(1)} %dynamic-slice.1), kind=kOutput, calls=%fused_computation.17 | convolution fusion | flops 25321472 | bytes 1008132 | tf_op jit(solution)/shard_map/dot_general | solution.py:56
  12.7 24.6 %all-gather = bf16[512,256]{1,0:T(8,128)(2,1)S(1)} all-gather(bf16[32,256]{1,0:T(8,128)(2,1)S(1)} %convolution_convert_fusion.2), channel_id=2, replica_groups=mesh['groups'=2,'seq'=8,'section'=2] {'seq','section'}, dimensions={0}, use_global_device_ids=true | all-gather | bytes 278528 | tf_op jit(solution)/shard_map/all_gather | solution.py:62
  37.3 0.4 fusion.18
  37.7 0.3 fusion.62
  38.3 0.3 fusion.19
  38.7 0.4 convolution_convert_fusion
  39.1 2.1 %all-gather.1 = bf16[128,1536]{1,0:T(8,128)(2,1)S(1)} all-gather(bf16[64,1536]{1,0:T(8,128)(2,1)S(1)} %convolution_convert_fusion), channel_id=3, replica_groups=mesh['groups'=2,'seq'=8,'section'=2] {'section'}, dimensions={0}, use_global_device_ids=true | all-gather | bytes 589824 | tf_op jit(solution)/shard_map/all_gather | solution.py:105
  41.6 0.5 convert_element_type.119
  42.4 0.4 fusion.24
  42.8 1.3 %collective-permute-start = (bf16[1,2,1536]{2,1,0:T(2,128)(2,1)S(1)}, bf16[1,2,1536]{2,1,0:T(2,128)(2,1)S(1)}, u32[]{:S(2)}, u32[]{:S(2)}) collective-permute-start(bf16[1,2,1536]{2,1,0:T(2,128)(2,1)S(1)} %get-tuple-element.8), channel_id=1, source_target_pairs={{0,2},{2,4},{4,6},{6,8},{8,10},{10,12},{12,14},{1,3},{3,5},{5,7},{... | collective-permute-start | bytes 18440 | tf_op jit(solution)/shard_map/ppermute | solution.py:17
  44.1 1.3 %collective-permute-start.1 = (bf16[1,2,1536]{2,1,0:T(2,128)(2,1)S(1)}, bf16[1,2,1536]{2,1,0:T(2,128)(2,1)S(1)}, u32[]{:S(2)}, u32[]{:S(2)}) collective-permute-start(bf16[1,2,1536]{2,1,0:T(2,128)(2,1)S(1)} %get-tuple-element.7), channel_id=1, source_target_pairs={{2,0},{4,2},{6,4},{8,6},{10,8},{12,10},{14,12},{3,1},{5,3},{7,5},{... | collective-permute-start | bytes 18440 | tf_op jit(solution)/shard_map/ppermute | solution.py:20
  45.4 0.9 fusion.35
  46.3 0.9 fusion.41
  47.2 1.1 constant_dynamic-update-slice_fusion
  48.4 1.3 %collective-permute-done.1 = bf16[1,2,1536]{2,1,0:T(2,128)(2,1)S(1)} collective-permute-done((bf16[1,2,1536]{2,1,0:T(2,128)(2,1)S(1)}, bf16[1,2,1536]{2,1,0:T(2,128)(2,1)S(1)}, u32[]{:S(2)}, u32[]{:S(2)}) %collective-permute-start.1) | collective-permute-done | bytes 6176 | tf_op jit(solution)/shard_map/ppermute | solution.py:20
  49.6 0.9 fusion.33
  50.5 0.9 fusion.40
  51.4 56.0 %all-gather.4.cloned.1.call-done = bf16[5,1536,384]{2,1,0:T(8,128)(2,1)} async-done(((bf16[5,192,384]{2,1,0:T(8,128)(2,1)}), bf16[5,1536,384]{2,1,0:T(8,128)(2,1)}) %all-gather.4.cloned.1.call-update) | async-done | bytes 5898256 | tf_op jit(solution)/shard_map/all_gather | solution.py:115
  107.4 5.1 %fusion.13 = bf16[1,128,384]{2,1,0:T(8,128)(2,1)} fusion(bf16[7680,384]{1,0:T(8,128)(2,1)} %bitcast.71, bf16[1,128,7680]{2,1,0:T(8,128)(2,1)} %fusion.40, bf16[1,128,1536]{2,1,0:T(8,128)(2,1)S(1)} %get-tuple-element.6, s32[]{:T(128)S(6)} %select_n.16, f32[384]{0:T(512)S(1)} %copy-done.5), kind=kOutput, calls=%fused_computation.10 | convolution fusion | flops 755171328 | bytes 8062468 | tf_op jit(solution)/shard_map/dot_general | solution.py:121
  (32 shorter events, 1.5 us)
Async XLA Ops:
  6.5 32.1 %copy-start = (bf16[512,1536]{1,0:T(8,128)(2,1)S(1)}, bf16[512,1536]{1,0:T(8,128)(2,1)}, u32[]{:S(2)}) copy-start(bf16[512,1536]{1,0:T(8,128)(2,1)} %param.14) | copy-start | bytes 4718596
  6.5 100.9 %all-gather.4.cloned.1.call-start = ((), (), s32[]{:S(2)}) async-start(), calls=%async_computation | async-start | bytes 6635520 | tf_op jit(solution)/shard_map/all_gather | solution.py:115
  9.4 1.7 %copy-start.3 = (f32[1536]{0:T(1024)S(1)}, f32[1536]{0:T(1024)}, u32[]{:S(2)}) copy-start(f32[1536]{0:T(1024)} %param.10) | copy-start | bytes 18436
  10.8 26.5 %copy-start.1 = (bf16[1536,512]{1,0:T(8,128)(2,1)S(1)}, bf16[1536,512]{1,0:T(8,128)(2,1)}, u32[]{:S(2)}) copy-start(bf16[1536,512]{1,0:T(8,128)(2,1)} %param.11) | copy-start | bytes 4718596
  41.2 1.0 copy-start.2
  41.3 1.1 copy-start.4
  42.8 2.6 %collective-permute-start = (bf16[1,2,1536]{2,1,0:T(2,128)(2,1)S(1)}, bf16[1,2,1536]{2,1,0:T(2,128)(2,1)S(1)}, u32[]{:S(2)}, u32[]{:S(2)}) collective-permute-start(bf16[1,2,1536]{2,1,0:T(2,128)(2,1)S(1)} %get-tuple-element.8), channel_id=1, source_target_pairs={{0,2},{2,4},{4,6},{6,8},{8,10},{10,12},{12,14},{1,3},{3,5},{5,7},{... | collective-permute-start | bytes 18440 | tf_op jit(solution)/shard_map/ppermute | solution.py:17
  44.1 5.5 %collective-permute-start.1 = (bf16[1,2,1536]{2,1,0:T(2,128)(2,1)S(1)}, bf16[1,2,1536]{2,1,0:T(2,128)(2,1)S(1)}, u32[]{:S(2)}, u32[]{:S(2)}) collective-permute-start(bf16[1,2,1536]{2,1,0:T(2,128)(2,1)S(1)} %get-tuple-element.7), channel_id=1, source_target_pairs={{2,0},{4,2},{6,4},{8,6},{10,8},{12,10},{14,12},{3,1},{5,3},{7,5},{... | collective-permute-start | bytes 18440 | tf_op jit(solution)/shard_map/ppermute | solution.py:20
  45.4 62.0 %copy-start.5 = (f32[384]{0:T(512)S(1)}, f32[384]{0:T(512)}, u32[]{:S(2)}) copy-start(f32[384]{0:T(512)} %param.17) | copy-start | bytes 4612
Sparse Core Ops, SparseCore 0:
  9.6 97.8 all-gather.3
